TPU v7x, 128 devices: a whole 4x4x4 slice. The times are simulated.
128 devices in a mesh: az: 16 (over z_hi, y, core), gz: 8 (over x, z_lo).
Axes of the slice: x: 4, y: 4, z: 4 (z_hi: 2, z_lo: 2; z = z_hi * 2 + z_lo), core: 2. Of those that a mesh axis runs over, the one named last changes fastest.
Arguments:
- starting_warmth: float32 [128, 512, 1024], P(None, 'az', 'gz'), may hold values from -6 to 6
- volume_transfer_multiplier: float32 [128, 512, 1024], P(None, 'az', 'gz'), may hold values from 0.005 to 4
- energy_supply_history: float32 [128, 512, 1024], P(None, 'az', 'gz'), may hold values from -1 to 2
Outputs:
- final_temperature: float32 [128, 512, 1024], P(None, 'az', 'gz')
All inputs are finite; a program needn't handle non-finite values.
Results may differ from a plain program's by a relative error of at most 0.0003.
Values sent between devices are 32-bit elements; how exact they have to be, the bound alone decides.
A program may use at most 128 MiB of HBM per device.

v0:
```python
import functools
import types

import jax
import jax.numpy as jnp
from jax import lax
from jax.experimental import pallas as pl
from jax.experimental.pallas import tpu as pltpu
from jax.sharding import PartitionSpec as P

STEPS = 2
PICARD = 2
diffusion_number = 1000.0
lengthwise_ratio = 0.048

MESH = pl.DeviceIdType.MESH
CELLS = 64
HALF = 32
ROWS = 64
TILES = 8
PART = 4
LANES = 128
VALUES = 7
GROUP = 16
STARTS = (0, 16, 32, 48)
ENDS = (16, 32, 48, 63)


def row_block(tile):
    return pl.ds(pl.multiple_of(tile * 8, 8), 8)


def conduct(field, factor):
    return factor * (1.5 + jnp.tanh(field))


def eliminate(ground, left, right, side):
    inverse = 1.0 / (ground + left + right)
    to_left = left * inverse
    to_right = right * inverse
    return to_left, to_right, side * inverse


def lane_at():
    return lax.broadcasted_iota(jnp.int32, (8, LANES), 1)


def twice_number(core, tile):
    rows = (lax.broadcasted_iota(jnp.int32, (8, LANES), 0) + (core * ROWS + tile * 8)).astype(jnp.float32)
    ratio = 128.0 / (128.0 + rows)
    return (2.0 * diffusion_number) * (ratio * ratio)


def first_rows(tile):
    rows = (lax.broadcasted_iota(jnp.int32, (8, LANES), 0) + tile * 8).astype(jnp.float32)
    ratio = 128.0 / (128.0 + rows)
    return (2.0 * diffusion_number) * (ratio * ratio)


def prepare(r, core, tile):
    rows = row_block(tile)
    lane_pair = lane_at() // 2
    number = first_rows(tile)
    packed = jnp.zeros((8, LANES), jnp.float32)
    packed_factor = jnp.zeros((8, LANES), jnp.float32)
    for cell in range(HALF):
        here = lane_pair == cell
        scaled = r.own_factor[cell, rows, :] * number
        r.scaled[cell, rows, :] = scaled
        packed = jnp.where(here, pltpu.roll(r.own_field[cell, rows, :], 2 * cell + 1, 1), packed)
        packed_factor = jnp.where(here, pltpu.roll(scaled, 2 * cell + 1, 1), packed_factor)
    r.own_ends[0, rows, :] = jnp.where(core == 0, packed, pltpu.roll(packed, 64, 1))
    r.own_ends[1, rows, :] = jnp.where(core == 0, packed_factor, pltpu.roll(packed_factor, 64, 1))


def merge(r, core, tile):
    rows = row_block(tile)
    low = lane_at() < 64
    ours = jnp.where(core == 0, jnp.where(low, 1, 0), jnp.where(low, 0, 1)) == 1
    held = pl.ds(pl.multiple_of(core * ROWS + tile * 8, 8), 8)
    r.ends[0, rows, :] = jnp.where(ours, r.own_ends[0, held, :], r.paired_ends[0, rows, :])
    r.factor_ends[rows, :] = jnp.where(ours, r.own_ends[1, held, :], r.paired_ends[1, rows, :])
    for side in range(2):
        r.near_ends[0, side, rows, :] = jnp.where(
            low, r.halves[side, 0, 0, rows, :], r.halves[side, 1, 0, rows, :]
        )
        r.near_factor[side, rows, :] = jnp.where(
            low, r.halves[side, 0, 1, rows, :], r.halves[side, 1, 1, rows, :]
        )


def border_of(r, core, low_gz, high_gz, step, tile):
    rows = row_block(tile)
    rate = (2.0 * lengthwise_ratio) / twice_number(core, tile)
    even = lax.rem(lane_at(), 2) == 0
    inside = jnp.where(even, high_gz, low_gz)
    ours = r.ends[step, rows, :]
    near = jnp.where(
        even,
        pltpu.roll(r.near_ends[step, 0, rows, :], LANES - 1, 1),
        pltpu.roll(r.near_ends[step, 1, rows, :], 1, 1),
    )
    near_factor = jnp.where(
        even,
        pltpu.roll(r.near_factor[0, rows, :], LANES - 1, 1),
        pltpu.roll(r.near_factor[1, rows, :], 1, 1),
    )
    our_k = conduct(ours, r.factor_ends[rows, :])
    near_k = conduct(near, near_factor)
    return rate * inside * our_k * near_k / (our_k + near_k) * (near - ours)


def explicit(number, field, factor, beyond, supply, rows, cells, store):
    rate = (2.0 * lengthwise_ratio) / number
    last = lane_at() == LANES - 1
    for group in range(0, cells, GROUP):
        at = range(group, group + GROUP)
        here = [field[cell, rows, :] for cell in at]
        k = [conduct(x, factor[cell, rows, :]) for cell, x in zip(at, here)]
        above = [pltpu.roll(x, LANES - 1, 1) for x in here]
        if beyond is None:
            k_above = [pltpu.roll(x, LANES - 1, 1) for x in k]
        else:
            k_above = [conduct(x, beyond[cell, rows, :]) for cell, x in zip(at, above)]
        flux = [
            jnp.where(last, 0.0, rate * k[i] * k_above[i] / (k[i] + k_above[i]) * (above[i] - here[i]))
            for i in range(GROUP)
        ]
        below = [pltpu.roll(x, 1, 1) for x in flux]
        for i, cell in enumerate(at):
            store(cell, here[i] + (flux[i] - below[i]) + supply[cell, rows, :])


def explicit_first(r, target, base, row_shift, tile):
    rows = row_block(tile)
    placed = pl.ds(pl.multiple_of(tile * 8 - row_shift, 8), 8)

    def store(cell, value):
        target[base + cell, placed, :] = value

    explicit(first_rows(tile), r.own_field, r.scaled, None, r.own_supply, rows, HALF, store)


def explicit_later(r, core, tile):
    rows = row_block(tile)

    def store(cell, value):
        r.raw[cell, rows, :] = value

    explicit(
        twice_number(core, tile), r.field, r.factor, r.beyond, r.supply, rows, CELLS, store
    )


def shift_factor(r, tile):
    rows = row_block(tile)
    for cell in range(CELLS):
        r.beyond[cell, rows, :] = pltpu.roll(r.factor[cell, rows, :], LANES - 1, 1)


def reduce_tile(r, border, tile):
    rows = row_block(tile)
    lane = lane_at()
    rim = jnp.logical_or(lane == 0, lane == LANES - 1)

    def k_of(cell):
        if border is None:
            return conduct(r.field[cell, rows, :], r.factor[cell, rows, :]), r.goal[cell, rows, :]
        edge = jnp.where(rim, pltpu.roll(border, LANES - 1 - 2 * cell, 1), 0.0)
        total = r.raw[cell, rows, :] + edge
        r.goal[cell, rows, :] = total
        return conduct(total, r.factor[cell, rows, :]), total

    heads = {start: k_of(start) for start in STARTS}
    first_k = heads[0][0]
    state = []
    for start in STARTS:
        after, after_side = k_of(start + 1)
        head_k = heads[start][0]
        link = head_k * after / (head_k + after)
        if start == 0:
            head_ground = jnp.ones((8, LANES), jnp.float32)
            head_side = heads[0][1]
        else:
            head_ground = jnp.zeros((8, LANES), jnp.float32)
            head_side = jnp.zeros((8, LANES), jnp.float32)
        state.append(
            (jnp.ones((8, LANES), jnp.float32), link, after_side, head_ground, head_side, after)
        )
    last_k = None
    for offset in range(1, 16):
        for chain, (start, end) in enumerate(zip(STARTS, ENDS)):
            cell = start + offset
            if cell >= end:
                continue
            ground, link, side, head_ground, head_side, k = state[chain]
            after, after_side = heads[cell + 1] if cell + 1 in heads else k_of(cell + 1)
            both = k + after
            product = k * after
            inverse = 1.0 / ((ground + link) * both + product)
            own = both * inverse
            ahead = product * inverse
            back = link * own
            r.to_next[cell, rows, :] = ahead
            r.to_sep[cell, rows, :] = back
            r.base[cell, rows, :] = side * own
            state[chain] = (
                1.0 + ground * ahead,
                link * ahead,
                after_side + side * ahead,
                head_ground + ground * back,
                head_side + side * back,
                after,
            )
            if cell + 1 == CELLS - 1:
                last_k = after
    ground_16 = state[0][0] + state[1][3]
    side_16 = state[0][2] + state[1][4]
    ground_32 = state[1][0] + state[2][3]
    side_32 = state[1][2] + state[2][4]
    ground_48 = state[2][0] + state[3][3]
    side_48 = state[2][2] + state[3][4]
    ground_0, side_0 = state[0][3], state[0][4]
    ground_63, side_63 = state[3][0], state[3][2]
    links = [part[1] for part in state]

    left, right, own = eliminate(ground_16, links[0], links[1], side_16)
    r.to_sep[16, rows, :] = left
    r.to_next[16, rows, :] = right
    r.base[16, rows, :] = own
    ground_0 += ground_16 * left
    side_0 += side_16 * left
    ground_32 += ground_16 * right
    side_32 += side_16 * right
    link_low = links[0] * right

    left, right, own = eliminate(ground_48, links[2], links[3], side_48)
    r.to_sep[48, rows, :] = left
    r.to_next[48, rows, :] = right
    r.base[48, rows, :] = own
    ground_32 += ground_48 * left
    side_32 += side_48 * left
    ground_63 += ground_48 * right
    side_63 += side_48 * right
    link_high = links[2] * right

    left, right, own = eliminate(ground_32, link_low, link_high, side_32)
    r.to_sep[32, rows, :] = left
    r.to_next[32, rows, :] = right
    r.base[32, rows, :] = own
    ground_0 += ground_32 * left
    side_0 += side_32 * left
    ground_63 += ground_32 * right
    side_63 += side_32 * right
    link = link_low * right
    for at, value in enumerate((link, ground_0, ground_63, side_0, side_63, first_k, last_k)):
        r.packet[tile, at] = value


def spread_tile(r, turn, pack_to, tile):
    rows = row_block(tile)
    x_first = r.returned[turn, tile, 0]
    x_last = r.returned[turn, tile, 1]
    lane_pair = lane_at() // 2
    packed = [jnp.zeros((8, LANES), jnp.float32)]

    def value(cell, sep, following):
        return (
            r.base[cell, rows, :]
            + r.to_sep[cell, rows, :] * sep
            + r.to_next[cell, rows, :] * following
        )

    def keep(cell, x):
        r.field[cell, rows, :] = x
        if pack_to is not None:
            packed[0] = jnp.where(lane_pair == cell, pltpu.roll(x, 2 * cell + 1, 1), packed[0])

    x_32 = value(32, x_first, x_last)
    x_16 = value(16, x_first, x_32)
    x_48 = value(48, x_32, x_last)
    seps = {0: x_first, 16: x_16, 32: x_32, 48: x_48, 63: x_last}
    for cell, x in seps.items():
        keep(cell, x)
    later = [seps[end] for end in ENDS]
    for offset in range(15, 0, -1):
        for chain, (start, end) in enumerate(zip(STARTS, ENDS)):
            cell = start + offset
            if cell >= end:
                continue
            later[chain] = value(cell, seps[start], later[chain])
            keep(cell, later[chain])
    if pack_to is not None:
        r.ends[pack_to, rows, :] = packed[0]


def close_ring(r, turn):
    parts = [[r.gathered[turn, member, at] for at in range(VALUES)] for member in range(TILES)]
    count = TILES
    ground = [part[2] for part in parts]
    side = [part[4] for part in parts]
    heads = []
    links = [None] * count
    for member in range(count):
        before = (member + count - 1) % count
        link, head_ground, _, head_side, _, head_k, _ = parts[member]
        tail_k = parts[before][6]
        both = tail_k + head_k
        product = tail_k * head_k
        inverse = 1.0 / ((head_ground + link) * both + product)
        own = both * inverse
        to_before = product * inverse
        to_last = link * own
        heads.append((to_before, to_last, head_side * own))
        links[member] = link * to_before
        ground[before] = ground[before] + head_ground * to_before
        side[before] = side[before] + head_side * to_before
        ground[member] = ground[member] + head_ground * to_last
        side[member] = side[member] + head_side * to_last
    undo = []
    nodes = list(range(count))
    while len(nodes) > 2:
        size = len(nodes)
        kept_links = []
        for at in range(1, size, 2):
            node, low, high = nodes[at], nodes[at - 1], nodes[(at + 1) % size]
            to_low, to_high, own = eliminate(ground[node], links[at], links[(at + 1) % size], side[node])
            undo.append((node, low, high, to_low, to_high, own))
            ground[low] = ground[low] + ground[node] * to_low
            side[low] = side[low] + side[node] * to_low
            ground[high] = ground[high] + ground[node] * to_high
            side[high] = side[high] + side[node] * to_high
            kept_links.append(links[at] * to_high)
        nodes = nodes[::2]
        links = kept_links[-1:] + kept_links[:-1]
    low, high = nodes
    link = links[0] + links[1]
    inverse = 1.0 / (ground[high] + link)
    to_low = link * inverse
    x = [None] * count
    x[low] = (side[low] + side[high] * to_low) / (ground[low] + ground[high] * to_low)
    x[high] = side[high] * inverse + to_low * x[low]
    for node, low, high, to_low, to_high, own in reversed(undo):
        x[node] = own + to_low * x[low] + to_high * x[high]
    for member in range(count):
        to_before, to_last, own = heads[member]
        r.answer[turn, member, 0] = own + to_before * x[(member + count - 1) % count] + to_last * x[member]
        r.answer[turn, member, 1] = x[member]


NAMES = (
    "field", "factor", "beyond", "supply", "raw", "goal", "to_sep", "to_next", "base",
    "own_field", "own_factor", "own_supply", "scaled", "stage",
    "own_ends", "paired_ends", "halves", "ends", "factor_ends", "near_ends", "near_factor",
    "packet", "gathered", "answer", "returned",
    "load_sem", "move_sem", "swap_send", "swap_recv", "first_send", "first_recv",
    "halo_send", "halo_recv", "packet_send", "packet_recv", "answer_send", "answer_recv",
    "out_sem", "out_send", "out_recv",
)


def kernel(warmth_hbm, factor_hbm, supply_hbm, out_hbm, *refs):
    r = types.SimpleNamespace(**dict(zip(NAMES, refs)))
    az = lax.axis_index("az")
    gz = lax.axis_index("gz")
    core = lax.rem(az, 2)
    chip = az // 2
    sibling = az + 1 - 2 * core
    gz_count = lax.axis_size("gz")
    across = gz + 1 - 2 * lax.rem(gz, 2)
    gz_up = lax.rem(gz + 1, gz_count)
    gz_down = lax.rem(gz + gz_count - 1, gz_count)
    other = lax.rem(gz + gz_count - 1 + 2 * lax.rem(gz, 2), gz_count)
    low_gz = jnp.where(gz > 0, 1.0, 0.0)
    high_gz = jnp.where(gz < gz_count - 1, 1.0, 0.0)

    barrier = pltpu.get_barrier_semaphore()
    for member in range(TILES):
        pl.semaphore_signal(
            barrier, inc=1, device_id=(2 * member + core, across), device_id_type=MESH
        )
    for where in ((sibling, gz), (az, other), (sibling, across), (sibling, other)):
        pl.semaphore_signal(barrier, inc=1, device_id=where, device_id_type=MESH)

    def for_range(low, high, work):
        def one(at, carry):
            work(at)
            return carry

        lax.fori_loop(low, high, one, 0)

    def remote(source, target, send_sem, recv_sem, where):
        return pltpu.make_async_remote_copy(
            src_ref=source, dst_ref=target, send_sem=send_sem, recv_sem=recv_sem,
            device_id=where, device_id_type=MESH,
        )

    def wait_for(ref, sem):
        pltpu.make_async_copy(ref, ref, sem).wait()

    loads = ((warmth_hbm, r.own_field), (factor_hbm, r.own_factor), (supply_hbm, r.own_supply))

    def load(cell):
        for at, (source, target) in enumerate(loads):
            pltpu.make_async_copy(source.at[:, cell], target.at[cell], r.load_sem.at[at]).start()

    for_range(0, HALF, load)
    for at in range(2):
        wait_for(loads[at][1], r.load_sem.at[at])

    own_rows = pl.ds(core * ROWS, ROWS)
    sent_rows = pl.ds((1 - core) * ROWS, ROWS)
    own_cells = pl.ds(core * HALF, HALF)
    sent_tile = (1 - core) * TILES
    own_tile = core * TILES

    for_range(sent_tile, sent_tile + TILES, functools.partial(prepare, r, core))
    pl.semaphore_wait(barrier, TILES + 4)
    factor_swap = remote(
        r.scaled.at[:, sent_rows], r.factor.at[own_cells],
        r.swap_send.at[0], r.swap_recv.at[0], (sibling, gz),
    )
    factor_swap.start()
    for_range(own_tile, own_tile + TILES, functools.partial(prepare, r, core))
    factor_move = pltpu.make_async_copy(
        r.scaled.at[:, own_rows], r.factor.at[own_cells], r.move_sem.at[0]
    )
    factor_move.start()
    firsts = []
    for side, where in enumerate((gz_down, gz_up)):
        for same in range(2):
            firsts.append(
                remote(
                    r.own_ends.at[:, own_rows if same else sent_rows],
                    r.halves.at[side, core],
                    r.first_send.at[2 * side + same],
                    r.first_recv.at[2 * side + core],
                    (az if same else sibling, where),
                )
            )
    firsts.append(
        remote(
            r.own_ends.at[:, sent_rows], r.paired_ends,
            r.first_send.at[4], r.first_recv.at[4], (sibling, gz),
        )
    )
    for copy in firsts:
        copy.start()
    wait_for(r.own_supply, r.load_sem.at[2])

    goal_swaps = []
    for chunk in range(2):
        low = sent_tile + PART * chunk
        for_range(
            low, low + PART,
            functools.partial(explicit_first, r, r.stage, 0, sent_tile * 8),
        )
        rows = pl.ds(PART * 8 * chunk, PART * 8)
        goal_swaps.append(
            remote(
                r.stage.at[:, rows], r.raw.at[own_cells, rows],
                r.swap_send.at[1 + chunk], r.swap_recv.at[1 + chunk], (sibling, gz),
            )
        )
        goal_swaps[-1].start()
    supply_swap = remote(
        r.own_supply.at[:, sent_rows], r.supply.at[own_cells],
        r.swap_send.at[3], r.swap_recv.at[3], (sibling, gz),
    )
    supply_swap.start()
    supply_move = pltpu.make_async_copy(
        r.own_supply.at[:, own_rows], r.supply.at[own_cells], r.move_sem.at[1]
    )
    supply_move.start()
    for_range(
        own_tile, own_tile + TILES,
        functools.partial(explicit_first, r, r.raw, core * HALF, own_tile * 8),
    )
    for side in range(2):
        for source in range(2):
            wait_for(r.halves.at[side, source], r.first_recv.at[2 * side + source])
    wait_for(r.paired_ends, r.first_recv.at[4])
    for_range(0, TILES, functools.partial(merge, r, core))
    factor_move.wait()
    factor_swap.wait_recv()

    y_at = lax.rem(chip, 4)

    def ordered(chunk, at):
        shift = jnp.where(at == 0, 2, jnp.where(at == 3, 0, 2 * at - 1))
        return PART * chunk + lax.rem(y_at + shift, 4)

    def forward(step, picard, chunk):
        turn = PICARD * step + picard

        def work(at):
            tile = ordered(chunk, at)
            border = None if picard else border_of(r, core, low_gz, high_gz, step, tile)
            reduce_tile(r, border, tile)
            remote(
                r.packet.at[tile], r.gathered.at[turn, chip],
                r.packet_send.at[turn], r.packet_recv.at[turn], (2 * tile + core, across),
            ).start()

        for_range(0, PART, work)

    def solve(turn):
        wait_for(r.gathered.at[turn], r.packet_recv.at[turn])
        close_ring(r, turn)

        def reply(at):
            member = ordered(lax.rem(at, 2), at // 2)
            remote(
                r.answer.at[turn, member], r.returned.at[turn, chip],
                r.answer_send.at[turn], r.answer_recv.at[turn, chip],
                (2 * member + core, across),
            ).start()

        for_range(0, TILES, reply)
        wait_for(r.packet, r.packet_send.at[turn])

    def backward(turn, chunk, pack_to):
        def work(at):
            tile = ordered(chunk, PART - 1 - at)
            wait_for(r.returned.at[turn, tile], r.answer_recv.at[turn, tile])
            spread_tile(r, turn, pack_to, tile)

        for_range(0, PART, work)

    halos = [[], []]
    for step in range(STEPS):
        for chunk in range(2):
            rows = pl.ds(PART * 8 * chunk, PART * 8)
            if step == 0:
                goal_swaps[chunk].wait_recv()
            else:
                low = PART * chunk
                for_range(low, low + PART, functools.partial(explicit_later, r, core))
                for copy in halos[chunk]:
                    copy.wait()
            forward(step, 0, chunk)
        if step == 0:
            for_range(0, TILES, functools.partial(shift_factor, r))
        for picard in range(PICARD):
            turn = PICARD * step + picard
            final = picard == PICARD - 1
            solve(turn)
            for chunk in range(2):
                last = step == STEPS - 1
                backward(turn, chunk, step + 1 if final and not last else None)
                if not final:
                    forward(step, picard + 1, chunk)
                elif not last:
                    rows = pl.ds(PART * 8 * chunk, PART * 8)
                    for side, where in enumerate((gz_down, gz_up)):
                        copy = remote(
                            r.ends.at[step + 1, rows], r.near_ends.at[step + 1, side, rows],
                            r.halo_send.at[chunk, side], r.halo_recv.at[chunk, side],
                            (az, where),
                        )
                        copy.start()
                        halos[chunk].append(copy)
            wait_for(r.answer.at[turn], r.answer_send.at[turn])
        if step == 0:
            supply_swap.wait_recv()
            supply_move.wait()

    def unload(cell):
        remote(
            r.field.at[(1 - core) * HALF + cell], out_hbm.at[own_rows, cell],
            r.out_send, r.out_recv, (sibling, gz),
        ).start()
        pltpu.make_async_copy(
            r.field.at[core * HALF + cell], out_hbm.at[own_rows, cell], r.out_sem
        ).start()

    for_range(0, HALF, unload)
    for copy in [factor_swap, supply_swap] + goal_swaps + firsts:
        copy.wait_send()
    whole = r.field.at[pl.ds(0, HALF)]
    wait_for(whole, r.out_sem)
    wait_for(whole, r.out_send)
    wait_for(whole, r.out_recv)


def shards(starting_warmth, volume_transfer_multiplier, energy_supply_history):
    def real(*shape):
        return pltpu.VMEM(shape + (LANES,), jnp.float32)

    cells = real(CELLS, ROWS)
    own = real(HALF, 2 * ROWS)
    dma = pltpu.SemaphoreType.DMA
    turns = STEPS * PICARD
    anywhere = pl.BlockSpec(memory_space=pltpu.HBM)
    return pl.pallas_call(
        kernel,
        out_shape=jax.ShapeDtypeStruct(starting_warmth.shape, jnp.float32),
        in_specs=[anywhere] * 3,
        out_specs=anywhere,
        scratch_shapes=[cells] * 9 + [own] * 4 + [
            real(HALF, ROWS),
            real(2, 2 * ROWS), real(2, ROWS), real(2, 2, 2, ROWS), real(STEPS, ROWS),
            real(ROWS), real(STEPS, 2, ROWS), real(2, ROWS),
            real(TILES, VALUES, 8), real(turns, TILES, VALUES, 8),
            real(turns, TILES, 2, 8), real(turns, TILES, 2, 8),
            dma((3,)), dma((2,)), dma((4,)), dma((4,)), dma((5,)), dma((5,)),
            dma((2, 2)), dma((2, 2)),
            dma((turns,)), dma((turns,)), dma((turns,)), dma((turns, TILES)),
            dma, dma, dma,
        ],
        compiler_params=pltpu.CompilerParams(
            collective_id=0, has_side_effects=True, vmem_limit_bytes=60 * 1024 * 1024
        ),
        name="annulus",
    )(starting_warmth, volume_transfer_multiplier, energy_supply_history)


def solution(mesh):
    placed = (P(None, "az", "gz"), P(None, "az", "gz"), P(None, "az", "gz"))
    return jax.shard_map(
        shards, mesh=mesh, in_specs=placed, out_specs=P(None, "az", "gz"), check_vma=False
    )
```

profile of v0, /device:TPU:1, one launch (start us, length us, event | category | flops | bytes accessed | tf_op | source)
XLA Modules:
  0.0 75.1 jit_solution(14205678023307835701)
XLA Ops:
  0.0 72.0 %annulus.1 = f32[128,32,128]{2,1,0:T(8,128)} custom-call(f32[128,32,128]{2,1,0:T(8,128)} %warmth_hbm.1, f32[128,32,128]{2,1,0:T(8,128)} %factor_hbm.1, f32[128,32,128]{2,1,0:T(8,128)} %supply_hbm.1), custom_call_target="tpu_custom_call" | custom-call | tf_op jit(solution)/shard_map/annulus/pallas_call | solution.py:595
  72.0 3.1 %copy.5 = f32[128,32,128]{2,1,0:T(8,128)} copy(f32[128,32,128]{2,1,0:T(8,128)} %annulus.1) | data formatting | bytes 4194304
where the time goes:
time: 75.2 us; the launch traced here: 75.1 us
  Pallas kernels  72 us (96%)
  local copies, waits for them, and re-layouts  3.08 us (4%)
    pallas_call x1, Pallas kernels, shards(): pl.pallas_call(kernel, out_shape=jax.ShapeDtypeStruct(starting_warmth.sha...  72 us
    unnamed x1, local copies, waits for them, and re-layouts  3.08 us

commit v1 on v0

--- a/solution.py
+++ b/solution.py
@@ -20,7 +20,7 @@
 TILES = 8
 PART = 4
 LANES = 128
-VALUES = 7
+VALUES = 5
 GROUP = 16
 STARTS = (0, 16, 32, 48)
 ENDS = (16, 32, 48, 63)
@@ -158,7 +158,7 @@
         r.beyond[cell, rows, :] = pltpu.roll(r.factor[cell, rows, :], LANES - 1, 1)
 
 
-def reduce_tile(r, border, tile):
+def reduce_tile(r, border, turn, tile):
     rows = row_block(tile)
     lane = lane_at()
     rim = jnp.logical_or(lane == 0, lane == LANES - 1)
@@ -253,14 +253,33 @@
     ground_63 += ground_32 * right
     side_63 += side_32 * right
     link = link_low * right
-    for at, value in enumerate((link, ground_0, ground_63, side_0, side_63, first_k, last_k)):
-        r.packet[tile, at] = value
+
+    to_face, to_last, own = eliminate(ground_0, first_k, link, side_0)
+    r.to_sep[0, rows, :] = to_face
+    r.to_next[0, rows, :] = to_last
+    r.base[0, rows, :] = own
+    ground_low = ground_0 * to_face
+    side_low = side_0 * to_face
+    ground_63 += ground_0 * to_last
+    side_63 += side_0 * to_last
+    link = first_k * to_last
+
+    to_low, to_high, own = eliminate(ground_63, link, last_k, side_63)
+    r.to_sep[63, rows, :] = to_low
+    r.to_next[63, rows, :] = to_high
+    r.base[63, rows, :] = own
+    ground_low += ground_63 * to_low
+    side_low += side_63 * to_low
+    link = link * to_high
+    faces = (link, ground_low, ground_63 * to_high, side_low, side_63 * to_high)
+    for at, value in enumerate(faces):
+        r.packet[turn, tile, at] = value
 
 
 def spread_tile(r, turn, pack_to, tile):
     rows = row_block(tile)
-    x_first = r.returned[turn, tile, 0]
-    x_last = r.returned[turn, tile, 1]
+    low_face = r.returned[turn, tile, 0]
+    high_face = r.returned[turn, tile, 1]
     lane_pair = lane_at() // 2
     packed = [jnp.zeros((8, LANES), jnp.float32)]
 
@@ -276,6 +295,8 @@
         if pack_to is not None:
             packed[0] = jnp.where(lane_pair == cell, pltpu.roll(x, 2 * cell + 1, 1), packed[0])
 
+    x_last = value(63, low_face, high_face)
+    x_first = value(0, low_face, x_last)
     x_32 = value(32, x_first, x_last)
     x_16 = value(16, x_first, x_32)
     x_48 = value(48, x_32, x_last)
@@ -297,26 +318,9 @@
 def close_ring(r, turn):
     parts = [[r.gathered[turn, member, at] for at in range(VALUES)] for member in range(TILES)]
     count = TILES
-    ground = [part[2] for part in parts]
-    side = [part[4] for part in parts]
-    heads = []
-    links = [None] * count
-    for member in range(count):
-        before = (member + count - 1) % count
-        link, head_ground, _, head_side, _, head_k, _ = parts[member]
-        tail_k = parts[before][6]
-        both = tail_k + head_k
-        product = tail_k * head_k
-        inverse = 1.0 / ((head_ground + link) * both + product)
-        own = both * inverse
-        to_before = product * inverse
-        to_last = link * own
-        heads.append((to_before, to_last, head_side * own))
-        links[member] = link * to_before
-        ground[before] = ground[before] + head_ground * to_before
-        side[before] = side[before] + head_side * to_before
-        ground[member] = ground[member] + head_ground * to_last
-        side[member] = side[member] + head_side * to_last
+    ground = [parts[at][1] + parts[at - 1][2] for at in range(count)]
+    side = [parts[at][3] + parts[at - 1][4] for at in range(count)]
+    links = [parts[at - 1][0] for at in range(count)]
     undo = []
     nodes = list(range(count))
     while len(nodes) > 2:
@@ -343,9 +347,8 @@
     for node, low, high, to_low, to_high, own in reversed(undo):
         x[node] = own + to_low * x[low] + to_high * x[high]
     for member in range(count):
-        to_before, to_last, own = heads[member]
-        r.answer[turn, member, 0] = own + to_before * x[(member + count - 1) % count] + to_last * x[member]
-        r.answer[turn, member, 1] = x[member]
+        r.answer[turn, member, 0] = x[member]
+        r.answer[turn, member, 1] = x[(member + 1) % count]
 
 
 NAMES = (
@@ -377,9 +380,9 @@
     barrier = pltpu.get_barrier_semaphore()
     for member in range(TILES):
         pl.semaphore_signal(
-            barrier, inc=1, device_id=(2 * member + core, across), device_id_type=MESH
-        )
-    for where in ((sibling, gz), (az, other), (sibling, across), (sibling, other)):
+            barrier, inc=1, device_id=(2 * member + 1 - core, across), device_id_type=MESH
+        )
+    for where in ((sibling, gz), (az, across), (az, other), (sibling, other)):
         pl.semaphore_signal(barrier, inc=1, device_id=where, device_id_type=MESH)
 
     def for_range(low, high, work):
@@ -486,9 +489,14 @@
 
     y_at = lax.rem(chip, 4)
 
+    def wrap(shift):
+        return jnp.where(y_at + shift >= 4, y_at + shift - 4, y_at + shift)
+
+    seats = [wrap(2), wrap(1), wrap(3), y_at]
+
     def ordered(chunk, at):
-        shift = jnp.where(at == 0, 2, jnp.where(at == 3, 0, 2 * at - 1))
-        return PART * chunk + lax.rem(y_at + shift, 4)
+        first = jnp.where(at == 0, seats[0], seats[1])
+        return PART * chunk + jnp.where(at < 2, first, jnp.where(at == 2, seats[2], seats[3]))
 
     def forward(step, picard, chunk):
         turn = PICARD * step + picard
@@ -496,10 +504,10 @@
         def work(at):
             tile = ordered(chunk, at)
             border = None if picard else border_of(r, core, low_gz, high_gz, step, tile)
-            reduce_tile(r, border, tile)
+            reduce_tile(r, border, turn, tile)
             remote(
-                r.packet.at[tile], r.gathered.at[turn, chip],
-                r.packet_send.at[turn], r.packet_recv.at[turn], (2 * tile + core, across),
+                r.packet.at[turn, tile], r.gathered.at[turn, chip],
+                r.packet_send.at[turn], r.packet_recv.at[turn], (2 * tile + 1 - core, across),
             ).start()
 
         for_range(0, PART, work)
@@ -508,16 +516,14 @@
         wait_for(r.gathered.at[turn], r.packet_recv.at[turn])
         close_ring(r, turn)
 
-        def reply(at):
-            member = ordered(lax.rem(at, 2), at // 2)
-            remote(
-                r.answer.at[turn, member], r.returned.at[turn, chip],
-                r.answer_send.at[turn], r.answer_recv.at[turn, chip],
-                (2 * member + core, across),
-            ).start()
-
-        for_range(0, TILES, reply)
-        wait_for(r.packet, r.packet_send.at[turn])
+        for seat in seats:
+            for half in range(2):
+                member = seat + 4 * half
+                remote(
+                    r.answer.at[turn, member], r.returned.at[turn, chip],
+                    r.answer_send.at[turn], r.answer_recv.at[turn, chip],
+                    (2 * member + 1 - core, across),
+                ).start()
 
     def backward(turn, chunk, pack_to):
         def work(at):
@@ -526,6 +532,22 @@
             spread_tile(r, turn, pack_to, tile)
 
         for_range(0, PART, work)
+
+    def unload(chunk):
+        rows = pl.ds(PART * 8 * chunk, PART * 8)
+        placed = pl.ds(core * ROWS + PART * 8 * chunk, PART * 8)
+
+        def one(cell):
+            target = out_hbm.at[placed, cell]
+            remote(
+                r.field.at[(1 - core) * HALF + cell, rows], target,
+                r.out_send, r.out_recv, (sibling, gz),
+            ).start()
+            pltpu.make_async_copy(
+                r.field.at[core * HALF + cell, rows], target, r.out_sem
+            ).start()
+
+        for_range(0, HALF, one)
 
     halos = [[], []]
     for step in range(STEPS):
@@ -550,7 +572,9 @@
                 backward(turn, chunk, step + 1 if final and not last else None)
                 if not final:
                     forward(step, picard + 1, chunk)
-                elif not last:
+                elif last:
+                    unload(chunk)
+                else:
                     rows = pl.ds(PART * 8 * chunk, PART * 8)
                     for side, where in enumerate((gz_down, gz_up)):
                         copy = remote(
@@ -560,23 +584,15 @@
                         )
                         copy.start()
                         halos[chunk].append(copy)
-            wait_for(r.answer.at[turn], r.answer_send.at[turn])
         if step == 0:
             supply_swap.wait_recv()
             supply_move.wait()
 
-    def unload(cell):
-        remote(
-            r.field.at[(1 - core) * HALF + cell], out_hbm.at[own_rows, cell],
-            r.out_send, r.out_recv, (sibling, gz),
-        ).start()
-        pltpu.make_async_copy(
-            r.field.at[core * HALF + cell], out_hbm.at[own_rows, cell], r.out_sem
-        ).start()
-
-    for_range(0, HALF, unload)
     for copy in [factor_swap, supply_swap] + goal_swaps + firsts:
         copy.wait_send()
+    for turn in range(STEPS * PICARD):
+        wait_for(r.packet.at[turn], r.packet_send.at[turn])
+        wait_for(r.answer.at[turn], r.answer_send.at[turn])
     whole = r.field.at[pl.ds(0, HALF)]
     wait_for(whole, r.out_sem)
     wait_for(whole, r.out_send)
@@ -601,7 +617,7 @@
             real(HALF, ROWS),
             real(2, 2 * ROWS), real(2, ROWS), real(2, 2, 2, ROWS), real(STEPS, ROWS),
             real(ROWS), real(STEPS, 2, ROWS), real(2, ROWS),
-            real(TILES, VALUES, 8), real(turns, TILES, VALUES, 8),
+            real(turns, TILES, VALUES, 8), real(turns, TILES, VALUES, 8),
             real(turns, TILES, 2, 8), real(turns, TILES, 2, 8),
             dma((3,)), dma((2,)), dma((4,)), dma((4,)), dma((5,)), dma((5,)),
             dma((2, 2)), dma((2, 2)),

time: 75.2 us -> 71.1 us (0.945)
  Pallas kernels: 72 us -> 67.8 us
    pallas_call x1, Pallas kernels: 72 us -> 67.8 us  [shards(): pl.pallas_call(kernel, out_shape=jax.ShapeDtypeStruct(starting_warmth.sha...]
where the time goes in v1:
time: 71.1 us; the launch traced here: 70.9 us
  Pallas kernels  67.8 us (95%)
  local copies, waits for them, and re-layouts  3.08 us (4%)
    pallas_call x1, Pallas kernels, shards(): pl.pallas_call(kernel, out_shape=jax.ShapeDtypeStruct(starting_warmth.sha...  67.8 us
    unnamed x1, local copies, waits for them, and re-layouts  3.08 us

profile of v1, /device:TPU:1, one launch (start us, length us, event | category | flops | bytes accessed | tf_op | source)
XLA Modules:
  0.0 70.9 jit_solution(16709874560768774714)
XLA Ops:
  0.0 67.8 %annulus.1 = f32[128,32,128]{2,1,0:T(8,128)} custom-call(f32[128,32,128]{2,1,0:T(8,128)} %warmth_hbm.1, f32[128,32,128]{2,1,0:T(8,128)} %factor_hbm.1, f32[128,32,128]{2,1,0:T(8,128)} %supply_hbm.1), custom_call_target="tpu_custom_call" | custom-call | tf_op jit(solution)/shard_map/annulus/pallas_call | solution.py:611
  67.8 3.1 %copy.5 = f32[128,32,128]{2,1,0:T(8,128)} copy(f32[128,32,128]{2,1,0:T(8,128)} %annulus.1) | data formatting | bytes 4194304

commit v2 on v1

--- a/solution.py
+++ b/solution.py
@@ -315,8 +315,8 @@
         r.ends[pack_to, rows, :] = packed[0]
 
 
-def close_ring(r, turn):
-    parts = [[r.gathered[turn, member, at] for at in range(VALUES)] for member in range(TILES)]
+def close_ring(r, turn, chunk):
+    parts = [[r.gathered[turn, chunk, member, at] for at in range(VALUES)] for member in range(TILES)]
     count = TILES
     ground = [parts[at][1] + parts[at - 1][2] for at in range(count)]
     side = [parts[at][3] + parts[at - 1][4] for at in range(count)]
@@ -347,8 +347,8 @@
     for node, low, high, to_low, to_high, own in reversed(undo):
         x[node] = own + to_low * x[low] + to_high * x[high]
     for member in range(count):
-        r.answer[turn, member, 0] = x[member]
-        r.answer[turn, member, 1] = x[(member + 1) % count]
+        r.answer[turn, chunk, member, 0] = x[member]
+        r.answer[turn, chunk, member, 1] = x[(member + 1) % count]
 
 
 NAMES = (
@@ -403,11 +403,13 @@
 
     loads = ((warmth_hbm, r.own_field), (factor_hbm, r.own_factor), (supply_hbm, r.own_supply))
 
-    def load(cell):
-        for at, (source, target) in enumerate(loads):
+    def load(arrays, cell):
+        for at in arrays:
+            source, target = loads[at]
             pltpu.make_async_copy(source.at[:, cell], target.at[cell], r.load_sem.at[at]).start()
 
-    for_range(0, HALF, load)
+    for_range(0, HALF, functools.partial(load, (0, 1)))
+    for_range(0, HALF, functools.partial(load, (2,)))
     for at in range(2):
         wait_for(loads[at][1], r.load_sem.at[at])
 
@@ -494,40 +496,48 @@
 
     seats = [wrap(2), wrap(1), wrap(3), y_at]
 
-    def ordered(chunk, at):
+    layer = lax.rem(gz, 2)
+    solves = chip // 4 == 1 - layer
+
+    def ordered(at):
         first = jnp.where(at == 0, seats[0], seats[1])
-        return PART * chunk + jnp.where(at < 2, first, jnp.where(at == 2, seats[2], seats[3]))
+        return jnp.where(at < 2, first, jnp.where(at == 2, seats[2], seats[3]))
 
     def forward(step, picard, chunk):
         turn = PICARD * step + picard
 
         def work(at):
-            tile = ordered(chunk, at)
+            seat = ordered(at)
+            tile = PART * chunk + seat
             border = None if picard else border_of(r, core, low_gz, high_gz, step, tile)
             reduce_tile(r, border, turn, tile)
             remote(
-                r.packet.at[turn, tile], r.gathered.at[turn, chip],
-                r.packet_send.at[turn], r.packet_recv.at[turn], (2 * tile + 1 - core, across),
+                r.packet.at[turn, tile], r.gathered.at[turn, chunk, chip],
+                r.packet_send.at[turn], r.packet_recv.at[turn, chunk],
+                (2 * (4 * layer + seat) + 1 - core, across),
             ).start()
 
         for_range(0, PART, work)
 
     def solve(turn):
-        wait_for(r.gathered.at[turn], r.packet_recv.at[turn])
-        close_ring(r, turn)
-
-        for seat in seats:
-            for half in range(2):
-                member = seat + 4 * half
-                remote(
-                    r.answer.at[turn, member], r.returned.at[turn, chip],
-                    r.answer_send.at[turn], r.answer_recv.at[turn, chip],
-                    (2 * member + 1 - core, across),
-                ).start()
+        @pl.when(solves)
+        def _():
+            for chunk in range(2):
+                wait_for(r.gathered.at[turn, chunk], r.packet_recv.at[turn, chunk])
+                close_ring(r, turn, chunk)
+                tile = PART * chunk + y_at
+                for seat in seats:
+                    for half in range(2):
+                        member = seat + 4 * half
+                        remote(
+                            r.answer.at[turn, chunk, member], r.returned.at[turn, tile],
+                            r.answer_send.at[turn], r.answer_recv.at[turn, tile],
+                            (2 * member + 1 - core, across),
+                        ).start()
 
     def backward(turn, chunk, pack_to):
         def work(at):
-            tile = ordered(chunk, PART - 1 - at)
+            tile = PART * chunk + ordered(PART - 1 - at)
             wait_for(r.returned.at[turn, tile], r.answer_recv.at[turn, tile])
             spread_tile(r, turn, pack_to, tile)
 
@@ -537,17 +547,19 @@
         rows = pl.ds(PART * 8 * chunk, PART * 8)
         placed = pl.ds(core * ROWS + PART * 8 * chunk, PART * 8)
 
-        def one(cell):
-            target = out_hbm.at[placed, cell]
+        def to_sibling(cell):
             remote(
-                r.field.at[(1 - core) * HALF + cell, rows], target,
+                r.field.at[(1 - core) * HALF + cell, rows], out_hbm.at[placed, cell],
                 r.out_send, r.out_recv, (sibling, gz),
             ).start()
+
+        def to_own(cell):
             pltpu.make_async_copy(
-                r.field.at[core * HALF + cell, rows], target, r.out_sem
+                r.field.at[core * HALF + cell, rows], out_hbm.at[placed, cell], r.out_sem
             ).start()
 
-        for_range(0, HALF, one)
+        for_range(0, HALF, to_sibling)
+        for_range(0, HALF, to_own)
 
     halos = [[], []]
     for step in range(STEPS):
@@ -592,7 +604,12 @@
         copy.wait_send()
     for turn in range(STEPS * PICARD):
         wait_for(r.packet.at[turn], r.packet_send.at[turn])
-        wait_for(r.answer.at[turn], r.answer_send.at[turn])
+
+    @pl.when(solves)
+    def _():
+        for turn in range(STEPS * PICARD):
+            wait_for(r.answer.at[turn], r.answer_send.at[turn])
+
     whole = r.field.at[pl.ds(0, HALF)]
     wait_for(whole, r.out_sem)
     wait_for(whole, r.out_send)
@@ -617,11 +634,11 @@
             real(HALF, ROWS),
             real(2, 2 * ROWS), real(2, ROWS), real(2, 2, 2, ROWS), real(STEPS, ROWS),
             real(ROWS), real(STEPS, 2, ROWS), real(2, ROWS),
-            real(turns, TILES, VALUES, 8), real(turns, TILES, VALUES, 8),
-            real(turns, TILES, 2, 8), real(turns, TILES, 2, 8),
+            real(turns, TILES, VALUES, 8), real(turns, 2, TILES, VALUES, 8),
+            real(turns, 2, TILES, 2, 8), real(turns, TILES, 2, 8),
             dma((3,)), dma((2,)), dma((4,)), dma((4,)), dma((5,)), dma((5,)),
             dma((2, 2)), dma((2, 2)),
-            dma((turns,)), dma((turns,)), dma((turns,)), dma((turns, TILES)),
+            dma((turns,)), dma((turns, 2)), dma((turns,)), dma((turns, TILES)),
             dma, dma, dma,
         ],
         compiler_params=pltpu.CompilerParams(

time: 71.1 us -> 69.7 us (0.980)
  Pallas kernels: 67.8 us -> 66.5 us
    pallas_call x1, Pallas kernels: 67.8 us -> 66.5 us  [shards(): pl.pallas_call(kernel, out_shape=jax.ShapeDtypeStruct(starting_warmth.sha...]
where the time goes in v2:
time: 69.7 us; the launch traced here: 69.6 us
  Pallas kernels  66.5 us (95%)
  local copies, waits for them, and re-layouts  3.08 us (4%)
    pallas_call x1, Pallas kernels, shards(): pl.pallas_call(kernel, out_shape=jax.ShapeDtypeStruct(starting_warmth.sha...  66.5 us
    unnamed x1, local copies, waits for them, and re-layouts  3.08 us

profile of v2, /device:TPU:1, one launch (start us, length us, event | category | flops | bytes accessed | tf_op | source)
XLA Modules:
  0.0 69.6 jit_solution(17161727671527016933)
XLA Ops:
  0.0 66.5 %annulus.1 = f32[128,32,128]{2,1,0:T(8,128)} custom-call(f32[128,32,128]{2,1,0:T(8,128)} %warmth_hbm.1, f32[128,32,128]{2,1,0:T(8,128)} %factor_hbm.1, f32[128,32,128]{2,1,0:T(8,128)} %supply_hbm.1), custom_call_target="tpu_custom_call" | custom-call | tf_op jit(solution)/shard_map/annulus/pallas_call | solution.py:628
  66.5 3.1 %copy.5 = f32[128,32,128]{2,1,0:T(8,128)} copy(f32[128,32,128]{2,1,0:T(8,128)} %annulus.1) | data formatting | bytes 4194304

commit v3 on v2

--- a/solution.py
+++ b/solution.py
@@ -472,11 +472,9 @@
         r.own_supply.at[:, sent_rows], r.supply.at[own_cells],
         r.swap_send.at[3], r.swap_recv.at[3], (sibling, gz),
     )
-    supply_swap.start()
     supply_move = pltpu.make_async_copy(
         r.own_supply.at[:, own_rows], r.supply.at[own_cells], r.move_sem.at[1]
     )
-    supply_move.start()
     for_range(
         own_tile, own_tile + TILES,
         functools.partial(explicit_first, r, r.raw, core * HALF, own_tile * 8),
@@ -574,11 +572,14 @@
                     copy.wait()
             forward(step, 0, chunk)
         if step == 0:
-            for_range(0, TILES, functools.partial(shift_factor, r))
+            supply_swap.start()
+            supply_move.start()
         for picard in range(PICARD):
             turn = PICARD * step + picard
             final = picard == PICARD - 1
             solve(turn)
+            if turn == 0:
+                for_range(0, TILES, functools.partial(shift_factor, r))
             for chunk in range(2):
                 last = step == STEPS - 1
                 backward(turn, chunk, step + 1 if final and not last else None)

time: 69.7 us -> 67.9 us (0.974)
  Pallas kernels: 66.5 us -> 64.7 us
    pallas_call x1, Pallas kernels: 66.5 us -> 64.7 us  [shards(): pl.pallas_call(kernel, out_shape=jax.ShapeDtypeStruct(starting_warmth.sha...]
where the time goes in v3:
time: 67.9 us; the launch traced here: 67.8 us
  Pallas kernels  64.7 us (95%)
  local copies, waits for them, and re-layouts  3.08 us (5%)
    pallas_call x1, Pallas kernels, shards(): pl.pallas_call(kernel, out_shape=jax.ShapeDtypeStruct(starting_warmth.sha...  64.7 us
    unnamed x1, local copies, waits for them, and re-layouts  3.08 us

profile of v3, /device:TPU:1, one launch (start us, length us, event | category | flops | bytes accessed | tf_op | source)
XLA Modules:
  0.0 67.8 jit_solution(16370712631910690886)
XLA Ops:
  0.0 64.7 %annulus.1 = f32[128,32,128]{2,1,0:T(8,128)} custom-call(f32[128,32,128]{2,1,0:T(8,128)} %warmth_hbm.1, f32[128,32,128]{2,1,0:T(8,128)} %factor_hbm.1, f32[128,32,128]{2,1,0:T(8,128)} %supply_hbm.1), custom_call_target="tpu_custom_call" | custom-call | tf_op jit(solution)/shard_map/annulus/pallas_call | solution.py:629
  64.7 3.1 %copy.5 = f32[128,32,128]{2,1,0:T(8,128)} copy(f32[128,32,128]{2,1,0:T(8,128)} %annulus.1) | data formatting | bytes 4194304
